TPU v7x, 128 devices: a whole 4x4x4 slice. The times are simulated.
128 devices in a mesh: seq: 8 (over z, core), head: 16 (over x, y).
Axes of the slice: x: 4, y: 4, z: 4, core: 2. Of those that a mesh axis runs over, the one named last changes fastest.
Arguments:
- query_raw: bfloat16 [8192, 8192], P('seq', 'head'), may hold values from -12 to 12
- key_raw: bfloat16 [8192, 8192], P('seq', 'head'), may hold values from -6 to 6
- value_raw: bfloat16 [8192, 8192], P('seq', 'head'), may hold values from -6 to 6
- query_gain: float32 [8192], P('head'), may hold values from 0.1 to 1.9
- log_decay: float32 [64, 8192], P('head', 'seq'), may hold values from -1.5 to 0
- out_grad: bfloat16 [8192, 8192], P('seq', 'head'), may hold values from -0.75 to 0.75
Outputs:
- query_raw_grad: bfloat16 [8192, 8192], P(('seq', 'head'))
- key_raw_grad: bfloat16 [8192, 8192], P(('seq', 'head'))
- value_raw_grad: bfloat16 [8192, 8192], P(('seq', 'head'))
All inputs are finite; a program needn't handle non-finite values.
Results may differ from a plain program's by a relative error of at most 0.0021.
Values may be sent and summed in bfloat16 or wider, within the bound.
No kernel may reach another device: no remote copies, remote signals or barrier semaphores. Data moves between devices by JAX's collectives and lax.ppermute only.
A program may use at most 128 MiB of HBM per device.

v0:
```python
import functools
import jax
import jax.numpy as jnp
from jax import lax
from jax.sharding import Mesh
from jax.sharding import PartitionSpec as P

D = 8192
BLOCK = 128
HEAD = ("head_0", "head_1")
SEQ = ("seq_0", "seq_1")
SEQ_HEAD = ("seq_0", "seq_1", "head_0", "head_1")
epsilon = 1e-06


def from_everyone(value, axis):
    length = lax.axis_size(axis)
    return lax.all_to_all(
        jnp.broadcast_to(value[None], (length, *value.shape)), axis, 0, 0, tiled=True
    )


def taken_together(value, axis):
    return from_everyone(value, axis).sum(axis=0)


def carried_in(value, axis, combine, identity):
    length, mine = (lax.axis_size(axis), lax.axis_index(axis))
    everything = jax.tree.map(lambda part: lax.all_gather(part, axis), value)
    start = jax.tree.map(
        lambda part, zero: jnp.broadcast_to(jnp.asarray(zero, part.dtype), part.shape),
        value,
        identity,
    )

    def lap(k, before):
        reached = k < mine
        new = combine(before, jax.tree.map(lambda part: part[k], everything))
        return jax.tree.map(lambda a, b: jnp.where(reached, a, b), new, before)

    return lax.fori_loop(0, length, lap, start)


def nothing_yet(value, identity):
    return jax.tree.map(
        lambda part, zero: jnp.zeros_like(part) + jnp.asarray(zero, part.dtype), value, identity
    )


def carried_in_2(value, axes, combine, identity):
    before = start = nothing_yet(value, identity)
    subtotal = value
    for axis in reversed(axes):
        length, mine = (lax.axis_size(axis), lax.axis_index(axis))
        pieces = jax.tree.map(lambda part: lax.all_gather(part, axis), subtotal)
        inside, subtotal = (start, start)
        for k in reversed(range(length)):
            passed = k > mine
            subtotal = combine(subtotal, jax.tree.map(lambda part: part[k], pieces))
            inside = jax.tree.map(lambda new, old: jnp.where(passed, new, old), subtotal, inside)
        before = combine(inside, before)
    return before


def by_axis(value, axes):
    return functools.reduce(lax.psum, axes, value)


def exact_prod(form, left, right):
    return jnp.einsum(form, left, right, precision=lax.Precision.HIGHEST)


def block_parts(queries, keys, gates):
    size = gates.shape[0]
    cumul = jnp.cumsum(gates)
    element_slot = lax.broadcasted_iota(jnp.int32, (size, size), 0)
    column = lax.broadcasted_iota(jnp.int32, (size, size), 1)
    causal = element_slot >= column
    strict = element_slot > column
    spread = jnp.where(causal, cumul[:, None] - cumul[None, :], 0.0)
    weights = jnp.where(causal, jnp.exp(spread), 0.0)
    lower = jnp.where(strict, 2.0 * weights * exact_prod("ik,jk->ij", keys, keys), 0.0)
    system = lower + jnp.eye(size, dtype=jnp.float32)
    mixing = 2.0 * weights * exact_prod("ik,jk->ij", queries, keys)
    start_decay = jnp.exp(cumul)
    end_decay = jnp.exp(cumul[-1] - cumul)
    return (system, mixing, start_decay, end_decay, start_decay[-1])


def solve_lower(system, target):
    return lax.linalg.triangular_solve(
        system, target, left_side=True, lower=True, unit_diagonal=True
    )


def block_forward(queries, keys, values, start_state, gates):
    system, mixing, start_decay, end_decay, total = block_parts(queries, keys, gates)
    target = values - start_decay[:, None] * exact_prod("ik,kv->iv", keys, start_state)
    fresh = solve_lower(system, target)
    outputs = start_decay[:, None] * exact_prod("ik,kv->iv", queries, start_state) + exact_prod(
        "ij,jv->iv", mixing, fresh
    )
    end_state = total * start_state + 2.0 * exact_prod(
        "ik,iv->kv", keys, end_decay[:, None] * fresh
    )
    return (outputs, end_state)


def block_maps(queries, keys, values, gates, grad_out):
    system, mixing, start_decay, end_decay, total = block_parts(queries, keys, gates)
    width = keys.shape[1]
    both = solve_lower(system, jnp.concatenate([values, start_decay[:, None] * keys], axis=1))
    initial_amount = both[:, : values.shape[1]]
    weight = both[:, values.shape[1] :]
    transition = total * jnp.eye(width, dtype=jnp.float32) - 2.0 * exact_prod(
        "ik,ij->kj", keys, end_decay[:, None] * weight
    )
    displacement = 2.0 * exact_prod("ik,iv->kv", keys, end_decay[:, None] * initial_amount)
    inner = exact_prod("ij,iv->jv", mixing, grad_out)
    adjoint = exact_prod("ik,iv->kv", start_decay[:, None] * queries, grad_out) - exact_prod(
        "jk,jv->kv", weight, inner
    )
    return (transition, displacement, adjoint)


def block_grads(queries, keys, values, start_state, gates, grad_out, end_grad):

    def forward(query_part, key_part, value_part):
        return block_forward(query_part, key_part, value_part, start_state, gates)

    _, pullback = jax.vjp(forward, queries, keys, values)
    return pullback((grad_out, end_grad))


def batched(function):
    return jax.vmap(jax.vmap(function))


def compose(earlier, later):
    return (
        exact_prod("hij,hjk->hik", later[0], earlier[0]),
        exact_prod("hij,hjk->hik", later[0], earlier[1]) + later[1],
    )


def per_device(query_raw, key_raw, value_raw, query_gain, log_decay, out_grad):
    rows, width = query_raw.shape
    heads = log_decay.shape[0]
    head_dim = width // heads
    blocks = rows // BLOCK
    raw_query = query_raw.astype(jnp.float32)
    squares = taken_together(jnp.sum(raw_query * raw_query, axis=1), HEAD)
    inv_rms = lax.rsqrt(squares / D + epsilon)
    normed = raw_query * inv_rms[:, None]
    scale = head_dim ** (-0.5)
    queries = normed * query_gain * scale
    raw_key = key_raw.astype(jnp.float32).reshape(rows, heads, head_dim)
    key_scale = lax.rsqrt(jnp.sum(raw_key * raw_key, axis=2, keepdims=True) + epsilon)
    keys = raw_key * key_scale

    def to_blocks(array):
        return array.reshape(blocks, BLOCK, heads, head_dim).transpose(2, 0, 1, 3)

    query_blocks = to_blocks(queries)
    key_blocks = to_blocks(keys)
    value_blocks = to_blocks(value_raw.astype(jnp.float32))
    grad_blocks = to_blocks(out_grad.astype(jnp.float32))
    gate_blocks = log_decay.reshape(heads, blocks, BLOCK)
    transitions, displacements, adjoints = batched(block_maps)(
        query_blocks, key_blocks, value_blocks, gate_blocks, grad_blocks
    )
    trans_seq = jnp.moveaxis(transitions, 1, 0)
    offset_seq = jnp.moveaxis(displacements, 1, 0)
    adjoint_seq = jnp.moveaxis(adjoints, 1, 0)
    identity = jnp.broadcast_to(jnp.eye(head_dim, dtype=jnp.float32), (heads, head_dim, head_dim))
    zeros = jnp.zeros((heads, head_dim, head_dim), jnp.float32)

    def gather_step(carry, item):
        return (compose(carry, item), None)

    (device_map, device_offset), _ = lax.scan(
        gather_step, (identity, zeros), (trans_seq, offset_seq)
    )

    def collect_adjoint(carry, item):
        matrix, term = item
        return (exact_prod("hji,hjk->hik", matrix, carry) + term, None)

    device_adjoint, _ = lax.scan(collect_adjoint, zeros, (trans_seq, adjoint_seq), reverse=True)
    _, incoming = carried_in((device_map, device_offset), SEQ, compose, (identity, zeros))
    back_map = jnp.swapaxes(device_map, 1, 2)
    _, outgoing = carried_in_2((back_map, device_adjoint), SEQ, compose, (identity, zeros))

    def advance(state_matrix, item):
        matrix, shift = item
        return (exact_prod("hij,hjk->hik", matrix, state_matrix) + shift, state_matrix)

    def retreat(adjoint_state, item):
        matrix, term = item
        return (exact_prod("hji,hjk->hik", matrix, adjoint_state) + term, adjoint_state)

    _, starts = lax.scan(advance, incoming, (trans_seq, offset_seq))
    _, ends = lax.scan(retreat, outgoing, (trans_seq, adjoint_seq), reverse=True)
    query_grad, key_grad, value_grad = batched(block_grads)(
        query_blocks,
        key_blocks,
        value_blocks,
        jnp.moveaxis(starts, 0, 1),
        gate_blocks,
        grad_blocks,
        jnp.moveaxis(ends, 0, 1),
    )

    def from_blocks(array):
        return array.transpose(1, 2, 0, 3).reshape(rows, width)

    key_grad_rows = key_grad.transpose(1, 2, 0, 3).reshape(rows, heads, head_dim)
    key_raw_grad = key_scale * (
        key_grad_rows - keys * jnp.sum(keys * key_grad_rows, axis=2, keepdims=True)
    )
    key_raw_grad = key_raw_grad.reshape(rows, width).astype(jnp.bfloat16)
    value_raw_grad = from_blocks(value_grad).astype(jnp.bfloat16)
    scaled = from_blocks(query_grad) * query_gain * scale
    correction = by_axis(jnp.sum(scaled * normed, axis=1), HEAD) / D
    query_raw_grad = (inv_rms[:, None] * (scaled - normed * correction[:, None])).astype(
        jnp.bfloat16
    )
    return (
        lax.all_to_all(query_raw_grad, HEAD, split_axis=0, concat_axis=1, tiled=True),
        lax.all_to_all(key_raw_grad, HEAD, split_axis=0, concat_axis=1, tiled=True),
        lax.all_to_all(value_raw_grad, HEAD, split_axis=0, concat_axis=1, tiled=True),
    )


def solution(mesh):
    split = Mesh(mesh.devices.reshape(4, 2, 4, 4), ("seq_0", "seq_1", "head_0", "head_1"))
    return jax.shard_map(
        per_device,
        mesh=split,
        in_specs=(P(SEQ, HEAD), P(SEQ, HEAD), P(SEQ, HEAD), P(HEAD), P(HEAD, SEQ), P(SEQ, HEAD)),
        out_specs=(P(SEQ_HEAD, None), P(SEQ_HEAD, None), P(SEQ_HEAD, None)),
        check_vma=False,
    )
```

profile of v0, /device:TPU:0, one launch (start us, length us, event | category | flops | bytes accessed | tf_op | source)
XLA Modules:
  0.0 694.1 jit_solution(8259316048077969374)
XLA Ops:
  24.6 6.5 add_bitcast_fusion.2
  31.1 315.8 %custom-call.8 = f32[4,8,1,128,128]{3,4,2,1,0:T(8,128)} custom-call(f32[4,8,1,128,128]{4,3,2,1,0:T(8,128)} %add_bitcast_fusion.2), custom_call_target="InvertDiagBlocksLowerTriangular" | custom-call | tf_op jit(solution)/shard_map/vmap(vmap())/triangular_solve | solution.py:91
  346.9 6.6 fusion.32
  353.5 5.4 multiply_bitcast_fusion.1
  367.2 22.9 %while.72 = (s32[]{:T(128)}, f32[4,128,128]{2,1,0:T(8,128)S(1)}, f32[4,128,128]{2,1,0:T(8,128)S(1)}, f32[8,4,128,128]{3,2,1,0:T(8,128)}, f32[8,4,128,128]{3,2,1,0:T(8,128)}, /*index=5*/s32[]{:T(128)}, s32[]{:T(128)}) while((s32[]{:T(128)}, f32[4,128,128]{2,1,0:T(8,128)S(1)}, f32[4,128,128]{2,1,0:T(8,128)S(1)}, ...), condition=%wide.region_5.6_spmd.clone, body=%wide.region_4.5_spmd.clone.sunk | while | flops 201457664 | bytes 2885218 | solution.py:181
  396.0 7.2 %all-to-all-start = ((f32[16,1,1024]{2,1,0:T(1,128)}), f32[16,1,1024]{2,1,0:T(1,128)}, u32[]{:S(2)}, u32[]{:S(2)}) async-start(f32[16,1,1024]{2,1,0:T(1,128)} %broadcast_in_dim.86), calls=%async_computation | async-start | bytes 131072 | tf_op jit(solution)/shard_map/all_to_all | solution.py:18
  419.0 27.4 %all-gather.11.cloned.1.call-done = f32[32,128,128]{2,1,0:T(8,128)} async-done(((f32[4,128,128]{2,1,0:T(8,128)}), f32[32,128,128]{2,1,0:T(8,128)}) %all-gather.11.cloned.1.call-update) | async-done | bytes 2097168 | tf_op jit(solution)/shard_map/all_gather | solution.py:29
  446.4 11.9 %while.73 = (s32[]{:T(128)}, f32[4,128,128]{2,1,0:T(8,128)S(1)}, s32[]{:T(128)}, f32[8,4,128,128]{3,2,1,0:T(8,128)}, f32[8,4,128,128]{3,2,1,0:T(8,128)}, /*index=5*/s32[]{:T(128)}, s32[]{:T(128)}) while((s32[]{:T(128)}, f32[4,128,128]{2,1,0:T(8,128)S(1)}, s32[]{:T(128)}, f32[8,4,128,128]{3,2,1,0:T(8,128)}, ...), condition=%wide.region_7.8_spmd.clone, body=%wide.region_6.7_spmd.clone.sunk | while | flops 100925440 | bytes 1837671 | solution.py:41
  459.9 18.0 %while.70 = (s32[]{:T(128)}, f32[4,128,128]{2,1,0:T(8,128)S(1)}, f32[8,4,128,128]{3,2,1,0:T(8,128)}, f32[8,4,128,128]{3,2,1,0:T(8,128)}, f32[8,4,128,128]{3,2,1,0:T(8,128)}, /*index=5*/s32[]{:T(128)}) while((s32[]{:T(128)}, f32[4,128,128]{2,1,0:T(8,128)S(1)}, f32[8,4,128,128]{3,2,1,0:T(8,128)}, f32[8,4,128,128]{3,2,1,0:T(8,128)}, ...), condition=%wide.region_9.10_spmd, body=%wide.region_8.9_spmd.sunk | while | flops 100728832 | bytes 2098257 | solution.py:202
  490.8 5.9 add_bitcast_fusion.1
  502.0 10.4 %psum.14 = f32[1024]{0:T(1024)S(1)} all-reduce(f32[1024]{0:T(1024)S(1)} %fusion.39), channel_id=1, replica_groups=mesh['seq_0'=4,'seq_1'=2,'head_0'=4,'head_1'=4] {'head_0'}, use_global_device_ids=true, to_apply=%region_11.12 | all-reduce | flops 1024 | bytes 8192 | tf_op jit(solution)/shard_map/psum | solution.py:66
  512.4 10.5 %psum.15 = f32[1024]{0:T(1024)S(1)} all-reduce(f32[1024]{0:T(1024)S(1)} %psum.14), channel_id=1, replica_groups=mesh['seq_0'=4,'seq_1'=2,'head_0'=4,'head_1'=4] {'head_1'}, use_global_device_ids=true, to_apply=%region_12.13 | all-reduce | flops 1024 | bytes 8192 | tf_op jit(solution)/shard_map/psum | solution.py:66
  531.0 6.2 fusion.53
  547.8 11.9 %while.74 = (s32[]{:T(128)}, f32[4,128,128]{2,1,0:T(8,128)S(1)}, f32[8,4,128,128]{2,3,1,0:T(8,128)}, f32[8,4,128,128]{3,2,1,0:T(8,128)}, s32[]{:T(128)}, /*index=5*/s32[]{:T(128)}, s32[]{:T(128)}) while((s32[]{:T(128)}, f32[4,128,128]{2,1,0:T(8,128)S(1)}, f32[8,4,128,128]{2,3,1,0:T(8,128)}, f32[8,4,128,128]{3,2,1,0:T(8,128)}, ...), condition=%wide.region_14.15_spmd.clone, body=%wide.region_13.14_spmd.clone.sunk | while | flops 100794368 | bytes 1574506 | solution.py:189
  571.6 7.1 %fusion.51 = f32[4,8,128,128]{3,2,1,0:T(8,128)} fusion(f32[4,8,128,128]{3,2,1,0:T(8,128)} %copy-done.27, f32[4,8,128,128]{2,1,3,0:T(8,128)} %bitcast.275), kind=kOutput, calls=%fused_computation.66 | convolution fusion | flops 805306368 | bytes 6291456 | tf_op jit(solution)/shard_map/vmap(vmap(transpose(jvp(ik,jk->ij))))/dot_general | solution.py:70
  578.8 5.5 all-gather.17.cloned.1.call-done
  590.5 17.6 %while.71 = (s32[]{:T(128)}, f32[4,128,128]{2,1,0:T(8,128)S(1)}, f32[8,4,128,128]{3,2,1,0:T(8,128)}, f32[8,4,128,128]{2,3,1,0:T(8,128)}, f32[8,4,128,128]{3,2,1,0:T(8,128)}, /*index=5*/s32[]{:T(128)}, s32[]{:T(128)}) while((s32[]{:T(128)}, f32[4,128,128]{2,1,0:T(8,128)S(1)}, f32[8,4,128,128]{3,2,1,0:T(8,128)}, ...), condition=%wide.region_16.17_spmd, body=%wide.region_15.16_spmd.sunk | while | flops 100728832 | bytes 2098269 | solution.py:203
  618.5 6.9 fusion.169
  625.4 5.8 fusion.84
  635.5 7.0 %all-to-all-start.3 = ((bf16[16,64,512]{2,1,0:T(8,128)(2,1)}), bf16[16,64,512]{2,1,0:T(8,128)(2,1)S(1)}, u32[]{:S(2)}, u32[]{:S(2)}) async-start(bf16[16,64,512]{2,1,0:T(8,128)(2,1)} %convert_element_type.53), calls=%async_computation.3 | async-start | bytes 2097152 | tf_op jit(solution)/shard_map/all_to_all | solution.py:231
  642.5 6.7 fusion.79
  651.5 6.1 multiply_reduce_fusion
  664.2 7.3 %all-to-all-start.2 = ((bf16[16,64,512]{2,1,0:T(8,128)(2,1)}), bf16[16,64,512]{2,1,0:T(8,128)(2,1)S(1)}, u32[]{:S(2)}, u32[]{:S(2)}) async-start(bf16[16,64,512]{2,1,0:T(8,128)(2,1)} %bitcast.36), calls=%async_computation.2 | async-start | bytes 2097152 | tf_op jit(solution)/shard_map/all_to_all | solution.py:230
  674.9 11.3 %all-to-all-done.2 = bf16[16,64,512]{2,1,0:T(8,128)(2,1)S(1)} async-done(((bf16[16,64,512]{2,1,0:T(8,128)(2,1)}), bf16[16,64,512]{2,1,0:T(8,128)(2,1)S(1)}, u32[]{:S(2)}, u32[]{:S(2)}) %all-to-all-start.2) | async-done | bytes 1048608 | tf_op jit(solution)/shard_map/all_to_all | solution.py:230
  (314 shorter events, 211.5 us)
Async XLA Ops:
  7.2 411.8 %all-gather.13.cloned.1.call-start = ((), (), s32[]{:S(2)}) async-start(), calls=%async_computation.5 | async-start | bytes 2359296 | tf_op jit(solution)/shard_map/all_gather | solution.py:29
  15.4 4.9 copy-start.13
  353.5 5.5 copy-start.1
  353.5 5.5 copy-start.53
  390.8 55.6 %all-gather.11.cloned.1.call-start = ((), (), s32[]{:S(2)}) async-start(), calls=%async_computation.4 | async-start | bytes 2359296 | tf_op jit(solution)/shard_map/all_gather | solution.py:29
  391.6 11.7 %copy-start.16 = (f32[4,128,128]{2,1,0:T(8,128)S(1)}, f32[4,128,128]{2,1,0:T(8,128)}, u32[]{:S(2)}) copy-start(f32[4,128,128]{2,1,0:T(8,128)} %copy-done.15) | copy-start | bytes 786436
  396.0 16.7 %all-to-all-start = ((f32[16,1,1024]{2,1,0:T(1,128)}), f32[16,1,1024]{2,1,0:T(1,128)}, u32[]{:S(2)}, u32[]{:S(2)}) async-start(f32[16,1,1024]{2,1,0:T(1,128)} %broadcast_in_dim.86), calls=%async_computation | async-start | bytes 131072 | tf_op jit(solution)/shard_map/all_to_all | solution.py:18
  403.2 175.5 %all-gather.15.cloned.1.call-start = ((), (), s32[]{:S(2)}) async-start(), calls=%async_computation.6 | async-start | bytes 1310720 | tf_op jit(solution)/shard_map/all_gather | solution.py:55
  408.2 176.1 %all-gather.17.cloned.1.call-start = ((), (), s32[]{:S(2)}) async-start(), calls=%async_computation.7 | async-start | bytes 1310720 | tf_op jit(solution)/shard_map/all_gather | solution.py:55
  412.7 78.0 %copy-start.22 = (bf16[8,128,4,128]{3,2,1,0:T(4,128)(2,1)}, bf16[8,128,4,128]{3,2,1,0:T(4,128)(2,1)S(1)}, u32[]{:S(2)}) copy-start(bf16[8,128,4,128]{3,2,1,0:T(4,128)(2,1)S(1)} %reshape.159) | copy-start | bytes 3145732
  531.0 6.2 copy-start.10
  531.0 6.2 copy-start.23
  547.8 14.6 %copy-start.21 = (f32[8,128,128]{2,1,0:T(8,128)S(1)}, f32[8,128,128]{2,1,0:T(8,128)}, u32[]{:S(2)}) copy-start(f32[8,128,128]{2,1,0:T(8,128)} %copy-done.20) | copy-start | bytes 1572868
  567.3 68.2 %all-to-all-start.1 = ((bf16[16,64,512]{2,1,0:T(8,128)(2,1)}), bf16[16,64,512]{2,1,0:T(8,128)(2,1)}, u32[]{:S(2)}, u32[]{:S(2)}) async-start(bf16[16,64,512]{2,1,0:T(8,128)(2,1)} %bitcast.21), calls=%async_computation.1 | async-start | bytes 2097152 | tf_op jit(solution)/shard_map/all_to_all | solution.py:229
  578.8 8.4 %copy-start.32 = (f32[16,128,128]{2,1,0:T(8,128)S(1)}, f32[16,128,128]{2,1,0:T(8,128)}, u32[]{:S(2)}) copy-start(f32[16,128,128]{2,1,0:T(8,128)} %all-gather.15.cloned.1.call-done) | copy-start | bytes 3145732
  618.5 6.9 copy-start.8
  618.5 6.9 copy-start.12
  625.4 5.8 copy-start.6
  625.4 5.8 copy-start.45
  625.4 5.8 copy-start.50
  625.4 5.8 copy-start.52
  635.5 28.8 %all-to-all-start.3 = ((bf16[16,64,512]{2,1,0:T(8,128)(2,1)}), bf16[16,64,512]{2,1,0:T(8,128)(2,1)S(1)}, u32[]{:S(2)}, u32[]{:S(2)}) async-start(bf16[16,64,512]{2,1,0:T(8,128)(2,1)} %convert_element_type.53), calls=%async_computation.3 | async-start | bytes 2097152 | tf_op jit(solution)/shard_map/all_to_all | solution.py:231
  642.5 6.7 copy-start.29
  664.2 22.0 %all-to-all-start.2 = ((bf16[16,64,512]{2,1,0:T(8,128)(2,1)}), bf16[16,64,512]{2,1,0:T(8,128)(2,1)S(1)}, u32[]{:S(2)}, u32[]{:S(2)}) async-start(bf16[16,64,512]{2,1,0:T(8,128)(2,1)} %bitcast.36), calls=%async_computation.2 | async-start | bytes 2097152 | tf_op jit(solution)/shard_map/all_to_all | solution.py:230
  (39 other events, 99.5 us)
Sparse Core Ops, SparseCore 0:
  390.9 27.9 all-gather.12
  420.7 25.6 all-gather.10
  448.1 24.5 all-gather.14
  564.0 20.2 all-gather.16
where the time goes:
time: 704 us; the launch traced here: 694 us
  other arithmetic  335 us (48%)
  matrix products  179 us (25%)
  local copies, waits for them, and re-layouts  62.9 us (9%)
  waiting for transfers between devices  48.4 us (7%)
  starting transfers between devices  26.1 us (4%)
  blocking collectives  25.8 us (4%)
  between operations  15 us (2%)
    another operation x4, other arithmetic, solve_lower(): lax.linalg.triangular_solve(system, target, left_side=True, lower=True, u...  317 us
    dot_general x76, matrix products, exact_prod(): return jnp.einsum(form, left, right, precision=lax.Precision.HIGHEST)  155 us
    all_gather x2, waiting for transfers between devices, carried_in(): everything = jax.tree.map(lambda part: lax.all_gather(part, axis), value)  30.9 us
    psum x2, blocking collectives, by_axis(): return functools.reduce(lax.psum, axes, value)  20.9 us
    unnamed x121, local copies, waits for them, and re-layouts  20.6 us
    another operation x4, matrix products, solve_lower(): lax.linalg.triangular_solve(system, target, left_side=True, lower=True, u...  17.1 us
  transfers between devices with their start and end apart: 8, of which 4 were waited for; matrix products, arithmetic and copies ran while one was open for 27% of the time, Pallas kernels for 0%

commit v1 on v0

--- a/solution.py
+++ b/solution.py
@@ -227,7 +227,12 @@
     )
     return (
         lax.all_to_all(query_raw_grad, HEAD, split_axis=0, concat_axis=1, tiled=True),
-        lax.all_to_all(key_raw_grad, HEAD, split_axis=0, concat_axis=1, tiled=True),
+        jnp.concatenate(
+            lax.all_to_all(
+                jnp.stack(jnp.split(key_raw_grad, lax.axis_size(HEAD), axis=0)), HEAD, 0, 0
+            ),
+            axis=1,
+        ),
         lax.all_to_all(value_raw_grad, HEAD, split_axis=0, concat_axis=1, tiled=True),
     )
 

time: 704 us -> 716 us (1.017)
  local copies, waits for them, and re-layouts: 62.9 us -> 74.7 us
  waiting for transfers between devices: 48.4 us -> 58.6 us
    unnamed x121 -> x128, local copies, waits for them, and re-layouts: 20.6 us -> 30.5 us
    all_to_all x1, waiting for transfers between devices: 0.01 us -> 8.84 us  [per_device(): lax.all_to_all(value_raw_grad, HEAD, split_axis=0, concat_axis=1, tiled=T...]
  transfers between devices with their start and end apart: 8 -> 8, of which waited for: 4 -> 5; matrix products, arithmetic and copies ran while one was open for 27% -> 28% of each run, Pallas kernels for 0% -> 0%
where the time goes in v1:
time: 716 us; the launch traced here: 705 us
  other arithmetic  335 us (47%)
  matrix products  172 us (24%)
  local copies, waits for them, and re-layouts  74.7 us (10%)
  waiting for transfers between devices  58.6 us (8%)
  blocking collectives  25.8 us (4%)
  starting transfers between devices  22.2 us (3%)
  between operations  14.9 us (2%)
    another operation x4, other arithmetic, solve_lower(): lax.linalg.triangular_solve(system, target, left_side=True, lower=True, u...  317 us
    dot_general x76, matrix products, exact_prod(): return jnp.einsum(form, left, right, precision=lax.Precision.HIGHEST)  151 us
    all_gather x2, waiting for transfers between devices, carried_in(): everything = jax.tree.map(lambda part: lax.all_gather(part, axis), value)  30.9 us
    unnamed x128, local copies, waits for them, and re-layouts  30.5 us
    psum x2, blocking collectives, by_axis(): return functools.reduce(lax.psum, axes, value)  20.9 us
    another operation x4, matrix products, solve_lower(): lax.linalg.triangular_solve(system, target, left_side=True, lower=True, u...  16 us
  transfers between devices with their start and end apart: 8, of which 5 were waited for; matrix products, arithmetic and copies ran while one was open for 28% of the time, Pallas kernels for 0%

profile of v1, /device:TPU:0, one launch (start us, length us, event | category | flops | bytes accessed | tf_op | source)
XLA Modules:
  0.0 705.2 jit_solution(7479147862705647702)
XLA Ops:
  24.5 6.5 add_bitcast_fusion.2
  31.0 315.8 %custom-call.8 = f32[4,8,1,128,128]{3,4,2,1,0:T(8,128)} custom-call(f32[4,8,1,128,128]{4,3,2,1,0:T(8,128)} %add_bitcast_fusion.2), custom_call_target="InvertDiagBlocksLowerTriangular" | custom-call | tf_op jit(solution)/shard_map/vmap(vmap())/triangular_solve | solution.py:91
  346.9 6.6 fusion.32
  353.5 5.4 multiply_bitcast_fusion.1
  358.9 4.7 bitcast_subtract_fusion
  367.2 22.9 %while.72 = (s32[]{:T(128)}, f32[4,128,128]{2,1,0:T(8,128)S(1)}, f32[4,128,128]{2,1,0:T(8,128)S(1)}, f32[8,4,128,128]{3,2,1,0:T(8,128)}, f32[8,4,128,128]{3,2,1,0:T(8,128)}, /*index=5*/s32[]{:T(128)}, s32[]{:T(128)}) while((s32[]{:T(128)}, f32[4,128,128]{2,1,0:T(8,128)S(1)}, f32[4,128,128]{2,1,0:T(8,128)S(1)}, ...), condition=%wide.region_5.6_spmd.clone, body=%wide.region_4.5_spmd.clone.sunk | while | flops 201457664 | bytes 2885218 | solution.py:181
  396.0 7.2 %all-to-all-start = ((f32[16,1,1024]{2,1,0:T(1,128)}), f32[16,1,1024]{2,1,0:T(1,128)}, u32[]{:S(2)}, u32[]{:S(2)}) async-start(f32[16,1,1024]{2,1,0:T(1,128)} %broadcast_in_dim.86), calls=%async_computation | async-start | bytes 131072 | tf_op jit(solution)/shard_map/all_to_all | solution.py:18
  419.0 27.5 %all-gather.11.cloned.1.call-done = f32[32,128,128]{2,1,0:T(8,128)} async-done(((f32[4,128,128]{2,1,0:T(8,128)}), f32[32,128,128]{2,1,0:T(8,128)}) %all-gather.11.cloned.1.call-update) | async-done | bytes 2097168 | tf_op jit(solution)/shard_map/all_gather | solution.py:29
  446.5 11.9 %while.73 = (s32[]{:T(128)}, f32[4,128,128]{2,1,0:T(8,128)S(1)}, s32[]{:T(128)}, f32[8,4,128,128]{3,2,1,0:T(8,128)}, f32[8,4,128,128]{3,2,1,0:T(8,128)}, /*index=5*/s32[]{:T(128)}, s32[]{:T(128)}) while((s32[]{:T(128)}, f32[4,128,128]{2,1,0:T(8,128)S(1)}, s32[]{:T(128)}, f32[8,4,128,128]{3,2,1,0:T(8,128)}, ...), condition=%wide.region_7.8_spmd.clone, body=%wide.region_6.7_spmd.clone.sunk | while | flops 100925440 | bytes 1837671 | solution.py:41
  459.9 18.0 %while.70 = (s32[]{:T(128)}, f32[4,128,128]{2,1,0:T(8,128)S(1)}, f32[8,4,128,128]{3,2,1,0:T(8,128)}, f32[8,4,128,128]{3,2,1,0:T(8,128)}, f32[8,4,128,128]{3,2,1,0:T(8,128)}, /*index=5*/s32[]{:T(128)}) while((s32[]{:T(128)}, f32[4,128,128]{2,1,0:T(8,128)S(1)}, f32[8,4,128,128]{3,2,1,0:T(8,128)}, f32[8,4,128,128]{3,2,1,0:T(8,128)}, ...), condition=%wide.region_9.10_spmd, body=%wide.region_8.9_spmd.sunk | while | flops 100728832 | bytes 2098257 | solution.py:202
  490.8 5.9 add_bitcast_fusion.1
  501.9 10.4 %psum.14 = f32[1024]{0:T(1024)S(1)} all-reduce(f32[1024]{0:T(1024)S(1)} %fusion.39), channel_id=1, replica_groups=mesh['seq_0'=4,'seq_1'=2,'head_0'=4,'head_1'=4] {'head_0'}, use_global_device_ids=true, to_apply=%region_11.12 | all-reduce | flops 1024 | bytes 8192 | tf_op jit(solution)/shard_map/psum | solution.py:66
  512.4 10.5 %psum.15 = f32[1024]{0:T(1024)S(1)} all-reduce(f32[1024]{0:T(1024)S(1)} %psum.14), channel_id=1, replica_groups=mesh['seq_0'=4,'seq_1'=2,'head_0'=4,'head_1'=4] {'head_1'}, use_global_device_ids=true, to_apply=%region_12.13 | all-reduce | flops 1024 | bytes 8192 | tf_op jit(solution)/shard_map/psum | solution.py:66
  530.9 6.2 fusion.53
  547.6 11.9 %while.74 = (s32[]{:T(128)}, f32[4,128,128]{2,1,0:T(8,128)S(1)}, f32[8,4,128,128]{2,3,1,0:T(8,128)}, f32[8,4,128,128]{3,2,1,0:T(8,128)}, s32[]{:T(128)}, /*index=5*/s32[]{:T(128)}, s32[]{:T(128)}) while((s32[]{:T(128)}, f32[4,128,128]{2,1,0:T(8,128)S(1)}, f32[8,4,128,128]{2,3,1,0:T(8,128)}, f32[8,4,128,128]{3,2,1,0:T(8,128)}, ...), condition=%wide.region_14.15_spmd.clone, body=%wide.region_13.14_spmd.clone.sunk | while | flops 100794368 | bytes 1574506 | solution.py:189
  571.5 7.2 %fusion.51 = f32[4,8,128,128]{3,2,1,0:T(8,128)} fusion(f32[4,8,128,128]{3,2,1,0:T(8,128)} %copy-done.24, f32[4,8,128,128]{2,1,3,0:T(8,128)} %bitcast.338), kind=kOutput, calls=%fused_computation.66 | convolution fusion | flops 805306368 | bytes 6291456 | tf_op jit(solution)/shard_map/vmap(vmap(transpose(jvp(ik,jk->ij))))/dot_general | solution.py:70
  578.7 5.5 all-gather.17.cloned.1.call-done
  590.4 17.6 %while.71 = (s32[]{:T(128)}, f32[4,128,128]{2,1,0:T(8,128)S(1)}, f32[8,4,128,128]{3,2,1,0:T(8,128)}, f32[8,4,128,128]{2,3,1,0:T(8,128)}, f32[8,4,128,128]{3,2,1,0:T(8,128)}, /*index=5*/s32[]{:T(128)}, s32[]{:T(128)}) while((s32[]{:T(128)}, f32[4,128,128]{2,1,0:T(8,128)S(1)}, f32[8,4,128,128]{3,2,1,0:T(8,128)}, ...), condition=%wide.region_16.17_spmd, body=%wide.region_15.16_spmd.sunk | while | flops 100728832 | bytes 2098269 | solution.py:203
  608.1 4.6 multiply_add_fusion
  617.1 4.5 fusion.185
  634.4 6.1 multiply_reduce_fusion
  655.8 6.8 all-to-all-start.3
  668.9 8.8 %all-to-all-done.3 = bf16[16,64,512]{2,1,0:T(8,128)(2,1)S(1)} async-done(((bf16[16,64,512]{2,1,0:T(8,128)(2,1)}), bf16[16,64,512]{2,1,0:T(8,128)(2,1)S(1)}, u32[]{:S(2)}, u32[]{:S(2)}) %all-to-all-start.3) | async-done | bytes 1048608 | tf_op jit(solution)/shard_map/all_to_all | solution.py:236
  684.8 12.6 %all-to-all-done.2 = bf16[16,64,512]{2,1,0:T(8,128)(2,1)S(1)} async-done(((bf16[16,64,512]{2,1,0:T(8,128)(2,1)}), bf16[16,64,512]{2,1,0:T(8,128)(2,1)S(1)}, u32[]{:S(2)}, u32[]{:S(2)}) %all-to-all-start.2) | async-done | bytes 1048608 | tf_op jit(solution)/shard_map/all_to_all | solution.py:231
  (322 shorter events, 225.7 us)
Async XLA Ops:
  7.2 411.8 %all-gather.13.cloned.1.call-start = ((), (), s32[]{:S(2)}) async-start(), calls=%async_computation.5 | async-start | bytes 2359296 | tf_op jit(solution)/shard_map/all_gather | solution.py:29
  10.0 4.7 copy-start.35
  15.4 4.9 copy-start.11
  353.5 5.5 copy-start.2
  353.5 5.5 copy-start.49
  390.8 55.7 %all-gather.11.cloned.1.call-start = ((), (), s32[]{:S(2)}) async-start(), calls=%async_computation.4 | async-start | bytes 2359296 | tf_op jit(solution)/shard_map/all_gather | solution.py:29
  391.5 11.7 %copy-start.14 = (f32[4,128,128]{2,1,0:T(8,128)S(1)}, f32[4,128,128]{2,1,0:T(8,128)}, u32[]{:S(2)}) copy-start(f32[4,128,128]{2,1,0:T(8,128)} %copy-done.13) | copy-start | bytes 786436
  396.0 16.7 %all-to-all-start = ((f32[16,1,1024]{2,1,0:T(1,128)}), f32[16,1,1024]{2,1,0:T(1,128)}, u32[]{:S(2)}, u32[]{:S(2)}) async-start(f32[16,1,1024]{2,1,0:T(1,128)} %broadcast_in_dim.86), calls=%async_computation | async-start | bytes 131072 | tf_op jit(solution)/shard_map/all_to_all | solution.py:18
  403.2 175.5 %all-gather.15.cloned.1.call-start = ((), (), s32[]{:S(2)}) async-start(), calls=%async_computation.6 | async-start | bytes 1310720 | tf_op jit(solution)/shard_map/all_gather | solution.py:55
  408.2 175.9 %all-gather.17.cloned.1.call-start = ((), (), s32[]{:S(2)}) async-start(), calls=%async_computation.7 | async-start | bytes 1310720 | tf_op jit(solution)/shard_map/all_gather | solution.py:55
  412.7 78.0 %copy-start.20 = (bf16[8,128,4,128]{3,2,1,0:T(4,128)(2,1)}, bf16[8,128,4,128]{3,2,1,0:T(4,128)(2,1)S(1)}, u32[]{:S(2)}) copy-start(bf16[8,128,4,128]{3,2,1,0:T(4,128)(2,1)S(1)} %reshape.164) | copy-start | bytes 3145732
  530.9 6.2 copy-start.8
  530.9 6.2 copy-start.21
  547.6 14.6 %copy-start.19 = (f32[8,128,128]{2,1,0:T(8,128)S(1)}, f32[8,128,128]{2,1,0:T(8,128)}, u32[]{:S(2)}) copy-start(f32[8,128,128]{2,1,0:T(8,128)} %copy-done.18) | copy-start | bytes 1572868
  559.5 4.2 copy-start.32
  559.5 4.2 copy-start.34
  562.6 4.5 copy-start.30
  567.1 88.7 %all-to-all-start.1 = ((bf16[16,64,512]{2,1,0:T(8,128)(2,1)}), bf16[16,64,512]{2,1,0:T(8,128)(2,1)}, u32[]{:S(2)}, u32[]{:S(2)}) async-start(bf16[16,64,512]{2,1,0:T(8,128)(2,1)} %bitcast.21), calls=%async_computation.1 | async-start | bytes 2097152 | tf_op jit(solution)/shard_map/all_to_all | solution.py:229
  578.7 8.4 %copy-start.28 = (f32[16,128,128]{2,1,0:T(8,128)S(1)}, f32[16,128,128]{2,1,0:T(8,128)}, u32[]{:S(2)}) copy-start(f32[16,128,128]{2,1,0:T(8,128)} %all-gather.15.cloned.1.call-done) | copy-start | bytes 3145732
  608.0 4.6 copy-start.7
  608.1 4.6 copy-start.10
  617.1 4.5 copy-start.5
  655.8 22.0 %all-to-all-start.3 = ((bf16[16,64,512]{2,1,0:T(8,128)(2,1)}), bf16[16,64,512]{2,1,0:T(8,128)(2,1)S(1)}, u32[]{:S(2)}, u32[]{:S(2)}) async-start(bf16[16,64,512]{2,1,0:T(8,128)(2,1)} %convert_element_type.53), calls=%async_computation.3 | async-start | bytes 2097152 | tf_op jit(solution)/shard_map/all_to_all | solution.py:236
  677.8 19.6 %all-to-all-start.2 = ((bf16[16,64,512]{2,1,0:T(8,128)(2,1)}), bf16[16,64,512]{2,1,0:T(8,128)(2,1)S(1)}, u32[]{:S(2)}, u32[]{:S(2)}) async-start(bf16[16,64,512]{2,1,0:T(8,128)(2,1)} %copy.368), calls=%async_computation.2 | async-start | bytes 2097152 | tf_op jit(solution)/shard_map/all_to_all | solution.py:231
  (35 other events, 75.9 us)
Sparse Core Ops, SparseCore 0:
  390.9 28.0 all-gather.12
  420.7 25.7 all-gather.10
  448.1 24.5 all-gather.14
  563.9 20.2 all-gather.16
